TPU v7x, 32 devices: a whole 2x2x4 slice. The times are simulated.
32 devices in a mesh: seg: 4 (over y, x), blk: 8 (over z, core).
Axes of the slice: x: 2, y: 2, z: 4, core: 2. Of those that a mesh axis runs over, the one named last changes fastest.
Arguments:
- psi_init: float32 [4, 128, 128, 128], P('seg', 'blk'), may hold values from -6 to 6
- env_left: bfloat16 [4, 48, 8, 128, 128], P('seg', 'blk'), may hold values from -0.5 to 0.5
- env_right: bfloat16 [4, 48, 8, 128, 128], P('seg', 'blk'), may hold values from -0.5 to 0.5
- coef: float32 [4, 48, 128], P('seg', 'blk'), may hold values from -1.25 to 1.25
- source: int32 [4, 48, 128], P('seg', 'blk'), may hold values from 0 to 127
- right_sector: int32 [4, 16, 8], P('seg'), may hold values from 0 to 7, each once within a row
- sector_sizes: int32 [4, 2, 8], P('seg'), may hold values from 32 to 128, as said below
- step_size: float32 [4], P('seg'), may hold values from 0.2 to 0.6
Outputs:
- psi: float32 [4, 128, 128, 128], P('seg', 'blk')
- energy: float32 [4], P('seg')
- density: float32 [4, 1024, 128], P('seg', 'blk')
Inputs may be any that keep to these rules, and one draw needn't show every extreme that they name: `sector_sizes`: in each row of 8 sizes one equals 128. `right_sector`: each row is a permutation of the sectors.
All inputs are finite; a program needn't handle non-finite values.
Results may differ from a plain program's by a relative error of at most 0.0018.
Values may be sent and summed in bfloat16 or wider, within the bound.
No kernel may reach another device: no remote copies, remote signals or barrier semaphores. Data moves between devices by JAX's collectives and lax.ppermute only.
A program may use at most 128 MiB of HBM per device.

v0:
```python
import jax
import jax.numpy as jnp
from jax import lax
from jax.sharding import PartitionSpec as P

NSEC = 8
BS = 128
P_SIZE = 16
ITERS = 3
NB = 128


def shifted_2(block, axis, distance):
    devices = range(lax.axis_size(axis))
    route = [(i - distance, i) for i in devices if i - distance in devices]
    return lax.ppermute(block, axis, route)


def block_mask(indices, sizes, right_flat):
    left_ids = indices % NSEC
    right_ids = jnp.take(right_flat, indices)
    positions = jnp.arange(BS, dtype=jnp.int32)
    row_live = positions[None, :] < jnp.take(sizes[0], left_ids)[:, None]
    col_live = positions[None, :] < jnp.take(sizes[1], right_ids)[:, None]
    return (row_live[:, :, None] & col_live[:, None, :]).astype(jnp.float32)


def apply_terms(full_bf, indices, left_env, right_env, weights, sources, right_flat):
    left_ids = indices % NSEC
    right_ids = jnp.take(right_flat, indices)

    def channel(accum, inputs):
        left_one, right_one, source_one, weight_one = inputs
        picked = jnp.take(full_bf, jnp.take(source_one, indices), axis=0)
        left_mats = jnp.take(left_one, left_ids, axis=0)
        middle = jnp.einsum(
            "nay,nyb->nab", left_mats, picked, preferred_element_type=jnp.float32
        ).astype(jnp.bfloat16)
        right_mats = jnp.take(right_one, right_ids, axis=0)
        result = jnp.einsum("nab,ncb->nac", middle, right_mats, preferred_element_type=jnp.float32)
        scaled = jnp.take(weight_one, indices)
        return (accum + scaled[:, None, None] * result, None)

    initial = jnp.zeros((indices.shape[0], BS, BS), jnp.float32)
    summed, _ = lax.scan(channel, initial, (left_env, right_env, sources, weights))
    return summed


def gram_parts(vector, indices, right_flat):
    left_ids = indices % NSEC
    right_ids = jnp.take(right_flat, indices)
    gram_left = jnp.einsum("nxb,nyb->nxy", vector, vector, precision=lax.Precision.HIGHEST)
    gram_right = jnp.einsum("nax,nay->nxy", vector, vector, precision=lax.Precision.HIGHEST)
    labels = jnp.arange(NSEC, dtype=jnp.int32)
    one_left = (left_ids[:, None] == labels[None, :]).astype(jnp.float32)
    one_right = (right_ids[:, None] == labels[None, :]).astype(jnp.float32)
    left_rho = jnp.einsum(
        "ns,nxy->sxy", one_left, gram_left, precision=lax.Precision.HIGHEST
    ).reshape(NSEC * BS, BS)
    right_rho = jnp.einsum(
        "ns,nxy->sxy", one_right, gram_right, precision=lax.Precision.HIGHEST
    ).reshape(NSEC * BS, BS)
    return (left_rho, right_rho)


def update_vector(current, applied, square_sum, cross_sum, image_sum, step_len, cells_total):
    quotient = cross_sum / square_sum
    new_norm = square_sum + step_len * step_len * (image_sum - quotient * quotient * square_sum)
    updated = (current - step_len * (applied - quotient * current)) * jnp.sqrt(
        cells_total / new_norm
    )
    return (updated, quotient)


def on_device(psi_init, env_left, env_right, coef, source, right_sector, sector_sizes, step_size):
    left_env = env_left[0]
    right_env = env_right[0]
    weights = coef[0]
    sources = source[0]
    right_flat = right_sector[0].reshape(NB)
    sizes = sector_sizes[0]
    step_len = step_size[0]
    own_count = psi_init.shape[1]
    cells_total = float(NB * BS * BS)
    own_ids = lax.axis_index("blk") * own_count + jnp.arange(own_count, dtype=jnp.int32)
    own_live = block_mask(own_ids, sizes, right_flat)
    current = psi_init[0] * own_live
    quotient = jnp.zeros((), jnp.float32)
    for iteration in range(ITERS):
        full_bf = lax.all_gather(current.astype(jnp.bfloat16), "blk", axis=0, tiled=True)

        def partial_terms(begin_row, row_count, full_bf=full_bf):
            indices = jnp.arange(row_count, dtype=jnp.int32)
            return apply_terms(full_bf, indices, left_env, right_env, weights, sources, right_flat)

        applied = (
            lax.psum_scatter(
                partial_terms(jnp.int32(0), own_count * lax.axis_size("blk")),
                "blk",
                scatter_dimension=0,
                tiled=True,
            )
            * own_live
        )
        square_sum, cross_sum, image_sum = lax.psum(
            (jnp.sum(current * current), jnp.sum(current * applied), jnp.sum(applied * applied)),
            "blk",
        )
        current, quotient = update_vector(
            current, applied, square_sum, cross_sum, image_sum, step_len, cells_total
        )
    left_part, right_part = gram_parts(current, own_ids, right_flat)
    left_rows, right_rows = (
        lax.psum_scatter(left_part, "blk", scatter_dimension=0, tiled=True),
        lax.psum_scatter(right_part, "blk", scatter_dimension=0, tiled=True),
    )
    shifted = shifted_2(right_rows, "seg", 1)
    density = (left_rows + shifted) / float(P_SIZE * BS)
    return (current[None], quotient.reshape(1), density[None])


def solution(mesh):
    in_specs = (
        P("seg", "blk", None, None),
        P("seg", "blk", None, None, None),
        P("seg", "blk", None, None, None),
        P("seg", "blk", None),
        P("seg", "blk", None),
        P("seg", None, None),
        P("seg", None, None),
        P("seg"),
    )
    out_specs = (P("seg", "blk", None, None), P("seg"), P("seg", "blk", None))
    return jax.shard_map(
        on_device, mesh=mesh, in_specs=in_specs, out_specs=out_specs, check_vma=False
    )
```

profile of v0, /device:TPU:0, one launch (start us, length us, event | category | flops | bytes accessed | tf_op | source)
XLA Modules:
  0.0 1026.9 jit_solution(6705878778556902143)
XLA Ops:
  16.2 47.1 %all-gather.4.cloned.1.call-done = bf16[128,128,128]{2,1,0:T(8,128)(2,1)} async-done(((bf16[16,128,128]{2,1,0:T(8,128)(2,1)}), bf16[128,128,128]{2,1,0:T(8,128)(2,1)}) %all-gather.4.cloned.1.call-update) | async-done | bytes 4194320 | tf_op jit(solution)/shard_map/all_gather | solution.py:90
  63.3 155.7 %while.36 = (s32[]{:T(128)}, f32[128,128,128]{2,1,0:T(8,128)}, f32[6,128]{1,0:T(8,128)S(1)}, bf16[6,8,128,128]{3,2,1,0:T(8,128)(2,1)S(1)}, s32[6,128]{1,0:T(8,12...) while((s32[]{:T(128)}, f32[128,128,128]{2,1,0:T(8,128)}, ...), condition=%wide.region_1.8_spmd.clone.clone, body=%wide.region_0.7_spmd.clone.clone.sunk | while | flops 1088431104 | bytes 55605632 | solution.py:45
  78.1 9.6 select_add_fusion.6
  102.6 11.4 %select_add_fusion.6 = f32[128,128,128]{2,1,0:T(8,128)} fusion(f32[128,128,128]{2,1,0:T(8,128)} %get-tuple-element.638, f32[128]{0:T(128)S(1)} %compare_select_fusion.30, pred[]{:T(512)S(6)} %compare.15, bf16[128,128,128]{2,1,0:T(8,128)(2,1)} %gather_fusion.1, pred[128]{0:T(512)(128)(4,1)S(1)} %get-tuple-element.592, ...), kind=kOutput, calls=%fused_computation.25.clone.1 | convolution fusion | flops 1088421888 | bytes 29361024 | tf_op jit(solution)/shard_map/while/body/eval_jaxpr/nab,ncb->nac/dot_general | solution.py:40
  128.8 11.4 %select_add_fusion.6 = f32[128,128,128]{2,1,0:T(8,128)} fusion(f32[128,128,128]{2,1,0:T(8,128)} %get-tuple-element.638, f32[128]{0:T(128)S(1)} %compare_select_fusion.30, pred[]{:T(512)S(6)} %compare.15, bf16[128,128,128]{2,1,0:T(8,128)(2,1)} %gather_fusion.1, pred[128]{0:T(512)(128)(4,1)S(1)} %get-tuple-element.592, ...), kind=kOutput, calls=%fused_computation.25.clone.1 | convolution fusion | flops 1088421888 | bytes 29361024 | tf_op jit(solution)/shard_map/while/body/eval_jaxpr/nab,ncb->nac/dot_general | solution.py:40
  155.1 11.4 %select_add_fusion.6 = f32[128,128,128]{2,1,0:T(8,128)} fusion(f32[128,128,128]{2,1,0:T(8,128)} %get-tuple-element.638, f32[128]{0:T(128)S(1)} %compare_select_fusion.30, pred[]{:T(512)S(6)} %compare.15, bf16[128,128,128]{2,1,0:T(8,128)(2,1)} %gather_fusion.1, pred[128]{0:T(512)(128)(4,1)S(1)} %get-tuple-element.592, ...), kind=kOutput, calls=%fused_computation.25.clone.1 | convolution fusion | flops 1088421888 | bytes 29361024 | tf_op jit(solution)/shard_map/while/body/eval_jaxpr/nab,ncb->nac/dot_general | solution.py:40
  181.4 11.4 %select_add_fusion.6 = f32[128,128,128]{2,1,0:T(8,128)} fusion(f32[128,128,128]{2,1,0:T(8,128)} %get-tuple-element.638, f32[128]{0:T(128)S(1)} %compare_select_fusion.30, pred[]{:T(512)S(6)} %compare.15, bf16[128,128,128]{2,1,0:T(8,128)(2,1)} %gather_fusion.1, pred[128]{0:T(512)(128)(4,1)S(1)} %get-tuple-element.592, ...), kind=kOutput, calls=%fused_computation.25.clone.1 | convolution fusion | flops 1088421888 | bytes 29361024 | tf_op jit(solution)/shard_map/while/body/eval_jaxpr/nab,ncb->nac/dot_general | solution.py:40
  207.6 11.4 %select_add_fusion.6 = f32[128,128,128]{2,1,0:T(8,128)} fusion(f32[128,128,128]{2,1,0:T(8,128)} %get-tuple-element.638, f32[128]{0:T(128)S(1)} %compare_select_fusion.30, pred[]{:T(512)S(6)} %compare.15, bf16[128,128,128]{2,1,0:T(8,128)(2,1)} %gather_fusion.1, pred[128]{0:T(512)(128)(4,1)S(1)} %get-tuple-element.592, ...), kind=kOutput, calls=%fused_computation.25.clone.1 | convolution fusion | flops 1088421888 | bytes 29361024 | tf_op jit(solution)/shard_map/while/body/eval_jaxpr/nab,ncb->nac/dot_general | solution.py:40
  219.8 87.7 %reduce-scatter.6.cloned.1.call-done = f32[16,128,128]{2,1,0:T(8,128)} async-done(((f32[128,128,128]{2,1,0:T(8,128)}), f32[16,128,128]{2,1,0:T(8,128)}) %reduce-scatter.6.cloned.1.call-update) | async-done | bytes 1048592 | tf_op jit(solution)/shard_map/reduce_scatter | solution.py:97
  309.7 14.3 %all-reduce.2 = (f32[]{:T(128)}, f32[]{:T(128)}, f32[]{:T(128)}) all-reduce(f32[]{:T(128)} %get-tuple-element.347, f32[]{:T(128)} %get-tuple-element.348, f32[]{:T(128)} %get-tuple-element.346), channel_id=1, replica_groups=mesh['seg'=4,'blk'=8] {'blk'}, use_global_device_ids=true, to_apply=%region_6.13 | all-reduce | flops 3 | bytes 24 | tf_op jit(solution)/shard_map/psum | solution.py:105
  329.9 45.3 %all-gather.6.cloned.1.call-done = bf16[128,128,128]{2,1,0:T(8,128)(2,1)} async-done(((bf16[16,128,128]{2,1,0:T(8,128)(2,1)}), bf16[128,128,128]{2,1,0:T(8,128)(2,1)}) %all-gather.6.cloned.1.call-update) | async-done | bytes 4194320 | tf_op jit(solution)/shard_map/all_gather | solution.py:90
  375.2 155.7 %while.37 = (s32[]{:T(128)}, f32[128,128,128]{2,1,0:T(8,128)}, f32[6,128]{1,0:T(8,128)S(1)}, bf16[6,8,128,128]{3,2,1,0:T(8,128)(2,1)S(1)}, s32[6,128]{1,0:T(8,12...) while((s32[]{:T(128)}, f32[128,128,128]{2,1,0:T(8,128)}, ...), condition=%wide.region_10.17_spmd.clone.clone, body=%wide.region_9.16_spmd.clone.clone.sunk | while | flops 1088431104 | bytes 55605632 | solution.py:45
  390.0 9.6 select_add_fusion.7
  414.5 11.4 %select_add_fusion.7 = f32[128,128,128]{2,1,0:T(8,128)} fusion(f32[128,128,128]{2,1,0:T(8,128)} %get-tuple-element.668, f32[128]{0:T(128)S(1)} %compare_select_fusion.32, pred[]{:T(512)S(6)} %compare.16, bf16[128,128,128]{2,1,0:T(8,128)(2,1)} %gather_fusion.6, pred[128]{0:T(512)(128)(4,1)S(1)} %get-tuple-element.607, ...), kind=kOutput, calls=%fused_computation.56.clone.1 | convolution fusion | flops 1088421888 | bytes 29361024 | tf_op jit(solution)/shard_map/while/body/eval_jaxpr/nab,ncb->nac/dot_general | solution.py:40
  440.7 11.4 %select_add_fusion.7 = f32[128,128,128]{2,1,0:T(8,128)} fusion(f32[128,128,128]{2,1,0:T(8,128)} %get-tuple-element.668, f32[128]{0:T(128)S(1)} %compare_select_fusion.32, pred[]{:T(512)S(6)} %compare.16, bf16[128,128,128]{2,1,0:T(8,128)(2,1)} %gather_fusion.6, pred[128]{0:T(512)(128)(4,1)S(1)} %get-tuple-element.607, ...), kind=kOutput, calls=%fused_computation.56.clone.1 | convolution fusion | flops 1088421888 | bytes 29361024 | tf_op jit(solution)/shard_map/while/body/eval_jaxpr/nab,ncb->nac/dot_general | solution.py:40
  467.0 11.4 %select_add_fusion.7 = f32[128,128,128]{2,1,0:T(8,128)} fusion(f32[128,128,128]{2,1,0:T(8,128)} %get-tuple-element.668, f32[128]{0:T(128)S(1)} %compare_select_fusion.32, pred[]{:T(512)S(6)} %compare.16, bf16[128,128,128]{2,1,0:T(8,128)(2,1)} %gather_fusion.6, pred[128]{0:T(512)(128)(4,1)S(1)} %get-tuple-element.607, ...), kind=kOutput, calls=%fused_computation.56.clone.1 | convolution fusion | flops 1088421888 | bytes 29361024 | tf_op jit(solution)/shard_map/while/body/eval_jaxpr/nab,ncb->nac/dot_general | solution.py:40
  493.2 11.4 %select_add_fusion.7 = f32[128,128,128]{2,1,0:T(8,128)} fusion(f32[128,128,128]{2,1,0:T(8,128)} %get-tuple-element.668, f32[128]{0:T(128)S(1)} %compare_select_fusion.32, pred[]{:T(512)S(6)} %compare.16, bf16[128,128,128]{2,1,0:T(8,128)(2,1)} %gather_fusion.6, pred[128]{0:T(512)(128)(4,1)S(1)} %get-tuple-element.607, ...), kind=kOutput, calls=%fused_computation.56.clone.1 | convolution fusion | flops 1088421888 | bytes 29361024 | tf_op jit(solution)/shard_map/while/body/eval_jaxpr/nab,ncb->nac/dot_general | solution.py:40
  519.5 11.4 %select_add_fusion.7 = f32[128,128,128]{2,1,0:T(8,128)} fusion(f32[128,128,128]{2,1,0:T(8,128)} %get-tuple-element.668, f32[128]{0:T(128)S(1)} %compare_select_fusion.32, pred[]{:T(512)S(6)} %compare.16, bf16[128,128,128]{2,1,0:T(8,128)(2,1)} %gather_fusion.6, pred[128]{0:T(512)(128)(4,1)S(1)} %get-tuple-element.607, ...), kind=kOutput, calls=%fused_computation.56.clone.1 | convolution fusion | flops 1088421888 | bytes 29361024 | tf_op jit(solution)/shard_map/while/body/eval_jaxpr/nab,ncb->nac/dot_general | solution.py:40
  530.9 88.4 %reduce-scatter.8.cloned.1.call-done = f32[16,128,128]{2,1,0:T(8,128)} async-done(((f32[128,128,128]{2,1,0:T(8,128)}), f32[16,128,128]{2,1,0:T(8,128)}) %reduce-scatter.8.cloned.1.call-update) | async-done | bytes 1048592 | tf_op jit(solution)/shard_map/reduce_scatter | solution.py:97
  621.5 14.3 %all-reduce.1 = (f32[]{:T(128)}, f32[]{:T(128)}, f32[]{:T(128)}) all-reduce(f32[]{:T(128)} %get-tuple-element.350, f32[]{:T(128)} %get-tuple-element.345, f32[]{:T(128)} %get-tuple-element.344), channel_id=1, replica_groups=mesh['seg'=4,'blk'=8] {'blk'}, use_global_device_ids=true, to_apply=%region_15.22 | all-reduce | flops 3 | bytes 24 | tf_op jit(solution)/shard_map/psum | solution.py:105
  641.8 45.1 %all-gather.8.cloned.1.call-done = bf16[128,128,128]{2,1,0:T(8,128)(2,1)} async-done(((bf16[16,128,128]{2,1,0:T(8,128)(2,1)}), bf16[128,128,128]{2,1,0:T(8,128)(2,1)}) %all-gather.8.cloned.1.call-update) | async-done | bytes 4194320 | tf_op jit(solution)/shard_map/all_gather | solution.py:90
  686.9 155.7 %while.38 = (s32[]{:T(128)}, f32[128,128,128]{2,1,0:T(8,128)}, f32[6,128]{1,0:T(8,128)S(1)}, bf16[6,8,128,128]{3,2,1,0:T(8,128)(2,1)S(1)}, s32[6,128]{1,0:T(8,12...) while((s32[]{:T(128)}, f32[128,128,128]{2,1,0:T(8,128)}, ...), condition=%wide.region_19.26_spmd.clone.clone, body=%wide.region_18.25_spmd.clone.clone.sunk | while | flops 1088431104 | bytes 55605632 | solution.py:45
  701.8 9.6 select_add_fusion.8
  726.2 11.4 %select_add_fusion.8 = f32[128,128,128]{2,1,0:T(8,128)} fusion(f32[128,128,128]{2,1,0:T(8,128)} %get-tuple-element.698, f32[128]{0:T(128)S(1)} %compare_select_fusion.34, pred[]{:T(512)S(6)} %compare.17, bf16[128,128,128]{2,1,0:T(8,128)(2,1)} %gather_fusion.11, pred[128]{0:T(512)(128)(4,1)S(1)} %get-tuple-element.622, ...), kind=kOutput, calls=%fused_computation.87.clone.1 | convolution fusion | flops 1088421888 | bytes 29361024 | tf_op jit(solution)/shard_map/while/body/eval_jaxpr/nab,ncb->nac/dot_general | solution.py:40
  752.5 11.4 %select_add_fusion.8 = f32[128,128,128]{2,1,0:T(8,128)} fusion(f32[128,128,128]{2,1,0:T(8,128)} %get-tuple-element.698, f32[128]{0:T(128)S(1)} %compare_select_fusion.34, pred[]{:T(512)S(6)} %compare.17, bf16[128,128,128]{2,1,0:T(8,128)(2,1)} %gather_fusion.11, pred[128]{0:T(512)(128)(4,1)S(1)} %get-tuple-element.622, ...), kind=kOutput, calls=%fused_computation.87.clone.1 | convolution fusion | flops 1088421888 | bytes 29361024 | tf_op jit(solution)/shard_map/while/body/eval_jaxpr/nab,ncb->nac/dot_general | solution.py:40
  778.7 11.4 %select_add_fusion.8 = f32[128,128,128]{2,1,0:T(8,128)} fusion(f32[128,128,128]{2,1,0:T(8,128)} %get-tuple-element.698, f32[128]{0:T(128)S(1)} %compare_select_fusion.34, pred[]{:T(512)S(6)} %compare.17, bf16[128,128,128]{2,1,0:T(8,128)(2,1)} %gather_fusion.11, pred[128]{0:T(512)(128)(4,1)S(1)} %get-tuple-element.622, ...), kind=kOutput, calls=%fused_computation.87.clone.1 | convolution fusion | flops 1088421888 | bytes 29361024 | tf_op jit(solution)/shard_map/while/body/eval_jaxpr/nab,ncb->nac/dot_general | solution.py:40
  805.0 11.4 %select_add_fusion.8 = f32[128,128,128]{2,1,0:T(8,128)} fusion(f32[128,128,128]{2,1,0:T(8,128)} %get-tuple-element.698, f32[128]{0:T(128)S(1)} %compare_select_fusion.34, pred[]{:T(512)S(6)} %compare.17, bf16[128,128,128]{2,1,0:T(8,128)(2,1)} %gather_fusion.11, pred[128]{0:T(512)(128)(4,1)S(1)} %get-tuple-element.622, ...), kind=kOutput, calls=%fused_computation.87.clone.1 | convolution fusion | flops 1088421888 | bytes 29361024 | tf_op jit(solution)/shard_map/while/body/eval_jaxpr/nab,ncb->nac/dot_general | solution.py:40
  831.2 11.4 %select_add_fusion.8 = f32[128,128,128]{2,1,0:T(8,128)} fusion(f32[128,128,128]{2,1,0:T(8,128)} %get-tuple-element.698, f32[128]{0:T(128)S(1)} %compare_select_fusion.34, pred[]{:T(512)S(6)} %compare.17, bf16[128,128,128]{2,1,0:T(8,128)(2,1)} %gather_fusion.11, pred[128]{0:T(512)(128)(4,1)S(1)} %get-tuple-element.622, ...), kind=kOutput, calls=%fused_computation.87.clone.1 | convolution fusion | flops 1088421888 | bytes 29361024 | tf_op jit(solution)/shard_map/while/body/eval_jaxpr/nab,ncb->nac/dot_general | solution.py:40
  842.7 88.4 %reduce-scatter.10.cloned.1.call-done = f32[16,128,128]{2,1,0:T(8,128)} async-done(((f32[128,128,128]{2,1,0:T(8,128)}), f32[16,128,128]{2,1,0:T(8,128)}) %reduce-scatter.10.cloned.1.call-update) | async-done | bytes 1048592 | tf_op jit(solution)/shard_map/reduce_scatter | solution.py:97
  933.2 14.3 %all-reduce = (f32[]{:T(128)}, f32[]{:T(128)}, f32[]{:T(128)}) all-reduce(f32[]{:T(128)} %get-tuple-element.349, f32[]{:T(128)} %get-tuple-element.343, f32[]{:T(128)} %get-tuple-element.342), channel_id=1, replica_groups=mesh['seg'=4,'blk'=8] {'blk'}, use_global_device_ids=true, to_apply=%region_24.31 | all-reduce | flops 3 | bytes 24 | tf_op jit(solution)/shard_map/psum | solution.py:105
  960.6 25.3 %reduce-scatter.14.cloned.1.call-done = f32[128,128]{1,0:T(8,128)} async-done(((f32[1024,128]{1,0:T(8,128)}), f32[128,128]{1,0:T(8,128)}) %reduce-scatter.14.cloned.1.call-update) | async-done | bytes 65552 | tf_op jit(solution)/shard_map/reduce_scatter | solution.py:115
  989.2 28.2 %reduce-scatter.12.cloned.1.call-done = f32[128,128]{1,0:T(8,128)} async-done(((f32[1024,128]{1,0:T(8,128)}), f32[128,128]{1,0:T(8,128)}) %reduce-scatter.12.cloned.1.call-update) | async-done | bytes 65552 | tf_op jit(solution)/shard_map/reduce_scatter | solution.py:114
  (375 shorter events, 301.3 us)
Async XLA Ops:
  7.2 56.1 %copy-start.1 = (bf16[1,6,8,128,128]{4,3,2,1,0:T(8,128)(2,1)S(1)}, bf16[1,6,8,128,128]{4,3,2,1,0:T(8,128)(2,1)}, u32[]{:S(2)}) copy-start(bf16[1,6,8,128,128]{4,3,2,1,0:T(8,128)(2,1)} %param.27) | copy-start | bytes 4718596
  7.2 56.1 %all-gather.4.cloned.1.call-start = ((), (), s32[]{:S(2)}) async-start(), calls=%async_computation.5 | async-start | bytes 4718592 | tf_op jit(solution)/shard_map/all_gather | solution.py:90
  9.6 53.7 %copy-start.4 = (s32[16]{0:T(128)}, s32[16]{0:T(128)S(1)}, u32[]{:S(2)}) copy-start(s32[16]{0:T(128)S(1)} %get-tuple-element.419) | copy-start | bytes 196
  13.5 294.0 %reduce-scatter.6.cloned.1.call-start = ((), (), s32[]{:S(2)}) async-start(), calls=%async_computation.6 | async-start | bytes 9437184 | tf_op jit(solution)/shard_map/reduce_scatter | solution.py:97
  219.0 88.5 %copy-start.3 = (f32[1,16,128,128]{3,2,1,0:T(8,128)S(1)}, f32[1,16,128,128]{3,2,1,0:T(8,128)}, u32[]{:S(2)}) copy-start(f32[1,16,128,128]{3,2,1,0:T(8,128)} %param.26) | copy-start | bytes 3145732
  219.0 156.1 %all-gather.6.cloned.1.call-start = ((), (), s32[]{:S(2)}) async-start(), calls=%async_computation.7 | async-start | bytes 4718592 | tf_op jit(solution)/shard_map/all_gather | solution.py:90
  329.8 289.6 %copy-start.2 = (f32[16,128,128]{2,1,0:T(8,128)}, f32[16,128,128]{2,1,0:T(8,128)S(1)}, u32[]{:S(2)}) copy-start(f32[16,128,128]{2,1,0:T(8,128)S(1)} %get-tuple-element.417) | copy-start | bytes 3145732
  329.8 289.5 %reduce-scatter.8.cloned.1.call-start = ((), (), s32[]{:S(2)}) async-start(), calls=%async_computation.8 | async-start | bytes 9437184 | tf_op jit(solution)/shard_map/reduce_scatter | solution.py:97
  530.9 156.0 %all-gather.8.cloned.1.call-start = ((), (), s32[]{:S(2)}) async-start(), calls=%async_computation.9 | async-start | bytes 4718592 | tf_op jit(solution)/shard_map/all_gather | solution.py:90
  641.6 289.5 %reduce-scatter.10.cloned.1.call-start = ((), (), s32[]{:S(2)}) async-start(), calls=%async_computation.10 | async-start | bytes 9437184 | tf_op jit(solution)/shard_map/reduce_scatter | solution.py:97
  842.6 143.2 %reduce-scatter.14.cloned.1.call-start = ((), (), s32[]{:S(2)}) async-start(), calls=%async_computation.12 | async-start | bytes 589824 | tf_op jit(solution)/shard_map/reduce_scatter | solution.py:115
  931.1 23.1 %copy-start.5 = (s32[16]{0:T(128)S(1)}, s32[16]{0:T(128)}, u32[]{:S(2)}) copy-start(s32[16]{0:T(128)} %copy-done.4) | copy-start | bytes 196
  952.4 6.2 copy-start
  956.2 61.3 %reduce-scatter.12.cloned.1.call-start = ((), (), s32[]{:S(2)}) async-start(), calls=%async_computation.11 | async-start | bytes 589824 | tf_op jit(solution)/shard_map/reduce_scatter | solution.py:114
  985.9 31.6 %collective-permute-start = (f32[128,128]{1,0:T(8,128)}, f32[128,128]{1,0:T(8,128)S(1)}, u32[]{:S(2)}, u32[]{:S(2)}) collective-permute-start(f32[128,128]{1,0:T(8,128)} %reduce-scatter.14.cloned.1.call-done), channel_id=1, source_target_pairs={{0,8},{8,16},{16,24},{1,9},{9,17},{17,25},{2,10},{10,18},{18,26},{... | collective-permute-start | bytes 196616 | tf_op jit(solution)/shard_map/ppermute | solution.py:16
Sparse Core Ops, SparseCore 0:
  13.6 49.5 all-gather.3
  219.2 88.3 reduce-scatter.5
  330.0 45.1 all-gather.5
  531.0 88.3 reduce-scatter.7
  641.7 45.1 all-gather.7
  842.8 88.3 reduce-scatter.9
  956.3 29.4 reduce-scatter.13
  988.1 29.2 reduce-scatter.11
where the time goes:
time: 1030 us
  waiting for transfers between devices  456 us (44%)
  local copies, waits for them, and re-layouts  273 us (27%)
  matrix products  206 us (20%)
  blocking collectives  42.9 us (4%)
  between operations  26.2 us (3%)
  other arithmetic  17.7 us (2%)
    reduce_scatter x3, waiting for transfers between devices, on_device(): lax.psum_scatter(partial_terms(jnp.int32(0), own_count * lax.axis_size('b...  265 us
    dot_general x18, matrix products, channel(): jnp.einsum('nab,ncb->nac', middle, right_mats, preferred_element_type=jnp...  199 us
    all_gather x3, waiting for transfers between devices, on_device(): lax.all_gather(current.astype(jnp.bfloat16), 'blk', axis=0, tiled=True)  137 us
    gather x36, local copies, waits for them, and re-layouts, channel(): picked = jnp.take(full_bf, jnp.take(source_one, indices), axis=0)  116 us
    gather x18, local copies, waits for them, and re-layouts, channel(): left_mats = jnp.take(left_one, left_ids, axis=0)  55 us
    gather x18, local copies, waits for them, and re-layouts, channel(): right_mats = jnp.take(right_one, right_ids, axis=0)  54.5 us
    psum x3, blocking collectives, on_device(): lax.psum((jnp.sum(current * current), jnp.sum(current * applied), jnp.sum...  42.9 us
    reduce_scatter x1, waiting for transfers between devices, on_device(): lax.psum_scatter(left_part, 'blk', scatter_dimension=0, tiled=True)  28.2 us
  transfers between devices with their start and end apart: 9, of which 8 were waited for; matrix products, arithmetic and copies ran while one was open for 1% of the time, Pallas kernels for 0%

commit v1 on v0

--- a/solution.py
+++ b/solution.py
@@ -87,7 +87,25 @@
     current = psi_init[0] * own_live
     quotient = jnp.zeros((), jnp.float32)
     for iteration in range(ITERS):
-        full_bf = lax.all_gather(current.astype(jnp.bfloat16), "blk", axis=0, tiled=True)
+        value = current.astype(jnp.bfloat16)
+        ways, here, step = (lax.axis_size("blk"), lax.axis_index("blk"), value.shape[0])
+        lengths = [n * ways if d == 0 else n for d, n in enumerate(value.shape)]
+        full_bf = lax.dynamic_update_slice_in_dim(
+            jnp.zeros(lengths, value.dtype), value, here * step, axis=0
+        )
+        going_up = going_down = value
+        for far in range(1, ways // 2 + 1):
+            going_up = lax.ppermute(going_up, "blk", [(d, (d + 1) % ways) for d in range(ways)])
+            full_bf = lax.dynamic_update_slice_in_dim(
+                full_bf, going_up, (here - far) % ways * step, axis=0
+            )
+            if 2 * far < ways:
+                going_down = lax.ppermute(
+                    going_down, "blk", [(d, (d - 1) % ways) for d in range(ways)]
+                )
+                full_bf = lax.dynamic_update_slice_in_dim(
+                    full_bf, going_down, (here + far) % ways * step, axis=0
+                )
 
         def partial_terms(begin_row, row_count, full_bf=full_bf):
             indices = jnp.arange(row_count, dtype=jnp.int32)

time: 1030 us -> 1050 us (1.019)
  waiting for transfers between devices: 456 us -> 406 us
  local copies, waits for them, and re-layouts: 273 us -> 315 us
  starting transfers between devices: 3.86 us -> 35.4 us
    all_gather x3 -> x0, waiting for transfers between devices: 137 us -> none  [on_device(): lax.all_gather(current.astype(jnp.bfloat16), 'blk', axis=0, tiled=True)]
    ppermute x0 -> x21, waiting for transfers between devices: none -> 85 us  [the longest x12 82 us: on_device(): lax.ppermute(going_up, 'blk', [(d, (d + 1) % ways) for d in range(ways)])]
    ppermute x0 -> x21, starting transfers between devices: none -> 31.8 us  [the longest x9 31.3 us: on_device(): lax.ppermute(going_down, 'blk', [(d, (d - 1) % ways) for d in range(ways)])]
    dynamic_update_slice x0 -> x21, local copies, waits for them, and re-layouts: none -> 31.5 us  [the longest x12 19.6 us: on_device(): lax.dynamic_update_slice_in_dim(full_bf, going_up, (here - far) % ways *...]
  transfers between devices with their start and end apart: 9 -> 27, of which waited for: 8 -> 20; matrix products, arithmetic and copies ran while one was open for 1% -> 3% of each run, Pallas kernels for 0% -> 0%
where the time goes in v1:
time: 1050 us
  waiting for transfers between devices  406 us (39%)
  local copies, waits for them, and re-layouts  315 us (30%)
  matrix products  206 us (20%)
  blocking collectives  43.2 us (4%)
  starting transfers between devices  35.4 us (3%)
  between operations  26.1 us (2%)
  other arithmetic  14 us (1%)
    reduce_scatter x3, waiting for transfers between devices, on_device(): lax.psum_scatter(partial_terms(jnp.int32(0), own_count * lax.axis_size('b...  268 us
    dot_general x18, matrix products, channel(): jnp.einsum('nab,ncb->nac', middle, right_mats, preferred_element_type=jnp...  200 us
    gather x36, local copies, waits for them, and re-layouts, channel(): picked = jnp.take(full_bf, jnp.take(source_one, indices), axis=0)  116 us
    ppermute x12, waiting for transfers between devices, on_device(): lax.ppermute(going_up, 'blk', [(d, (d + 1) % ways) for d in range(ways)])  82 us
    gather x18, local copies, waits for them, and re-layouts, channel(): right_mats = jnp.take(right_one, right_ids, axis=0)  55.3 us
    gather x18, local copies, waits for them, and re-layouts, channel(): left_mats = jnp.take(left_one, left_ids, axis=0)  54.5 us
    psum x3, blocking collectives, on_device(): lax.psum((jnp.sum(current * current), jnp.sum(current * applied), jnp.sum...  43.2 us
    ppermute x9, starting transfers between devices, on_device(): lax.ppermute(going_down, 'blk', [(d, (d - 1) % ways) for d in range(ways)])  31.3 us
  transfers between devices with their start and end apart: 27, of which 20 were waited for; matrix products, arithmetic and copies ran while one was open for 3% of the time, Pallas kernels for 0%

profile of v1, /device:TPU:0, one launch (start us, length us, event | category | flops | bytes accessed | tf_op | source)
XLA Modules:
  0.0 1048.2 jit_solution(17981652777255554392)
XLA Ops:
  19.9 9.9 collective-permute-done
  66.0 156.2 %while.36 = (s32[]{:T(128)}, f32[128,128,128]{2,1,0:T(8,128)}, f32[6,128]{1,0:T(8,128)S(1)}, bf16[6,8,128,128]{3,2,1,0:T(8,128)(2,1)S(1)}, s32[6,128]{1,0:T(8,12...) while((s32[]{:T(128)}, f32[128,128,128]{2,1,0:T(8,128)}, ...), condition=%wide.region_1.8_spmd.clone.clone, body=%wide.region_0.7_spmd.clone.clone.sunk | while | flops 1088431104 | bytes 55605624 | solution.py:45
  80.9 9.6 select_add_fusion.6
  105.4 11.4 %select_add_fusion.6 = f32[128,128,128]{2,1,0:T(8,128)} fusion(f32[128,128,128]{2,1,0:T(8,128)} %get-tuple-element.642, f32[128]{0:T(128)S(1)} %compare_select_fusion.30, pred[]{:T(512)S(6)} %compare.22, bf16[128,128,128]{2,1,0:T(8,128)(2,1)} %gather_fusion.1, pred[128]{0:T(512)(128)(4,1)S(1)} %get-tuple-element.596, ...), kind=kOutput, calls=%fused_computation.25.clone.1 | convolution fusion | flops 1088421888 | bytes 29361024 | tf_op jit(solution)/shard_map/while/body/eval_jaxpr/nab,ncb->nac/dot_general | solution.py:40
  131.7 11.4 %select_add_fusion.6 = f32[128,128,128]{2,1,0:T(8,128)} fusion(f32[128,128,128]{2,1,0:T(8,128)} %get-tuple-element.642, f32[128]{0:T(128)S(1)} %compare_select_fusion.30, pred[]{:T(512)S(6)} %compare.22, bf16[128,128,128]{2,1,0:T(8,128)(2,1)} %gather_fusion.1, pred[128]{0:T(512)(128)(4,1)S(1)} %get-tuple-element.596, ...), kind=kOutput, calls=%fused_computation.25.clone.1 | convolution fusion | flops 1088421888 | bytes 29361024 | tf_op jit(solution)/shard_map/while/body/eval_jaxpr/nab,ncb->nac/dot_general | solution.py:40
  158.0 11.4 %select_add_fusion.6 = f32[128,128,128]{2,1,0:T(8,128)} fusion(f32[128,128,128]{2,1,0:T(8,128)} %get-tuple-element.642, f32[128]{0:T(128)S(1)} %compare_select_fusion.30, pred[]{:T(512)S(6)} %compare.22, bf16[128,128,128]{2,1,0:T(8,128)(2,1)} %gather_fusion.1, pred[128]{0:T(512)(128)(4,1)S(1)} %get-tuple-element.596, ...), kind=kOutput, calls=%fused_computation.25.clone.1 | convolution fusion | flops 1088421888 | bytes 29361024 | tf_op jit(solution)/shard_map/while/body/eval_jaxpr/nab,ncb->nac/dot_general | solution.py:40
  184.4 11.4 %select_add_fusion.6 = f32[128,128,128]{2,1,0:T(8,128)} fusion(f32[128,128,128]{2,1,0:T(8,128)} %get-tuple-element.642, f32[128]{0:T(128)S(1)} %compare_select_fusion.30, pred[]{:T(512)S(6)} %compare.22, bf16[128,128,128]{2,1,0:T(8,128)(2,1)} %gather_fusion.1, pred[128]{0:T(512)(128)(4,1)S(1)} %get-tuple-element.596, ...), kind=kOutput, calls=%fused_computation.25.clone.1 | convolution fusion | flops 1088421888 | bytes 29361024 | tf_op jit(solution)/shard_map/while/body/eval_jaxpr/nab,ncb->nac/dot_general | solution.py:40
  210.7 11.4 %select_add_fusion.6 = f32[128,128,128]{2,1,0:T(8,128)} fusion(f32[128,128,128]{2,1,0:T(8,128)} %get-tuple-element.642, f32[128]{0:T(128)S(1)} %compare_select_fusion.30, pred[]{:T(512)S(6)} %compare.22, bf16[128,128,128]{2,1,0:T(8,128)(2,1)} %gather_fusion.1, pred[128]{0:T(512)(128)(4,1)S(1)} %get-tuple-element.596, ...), kind=kOutput, calls=%fused_computation.25.clone.1 | convolution fusion | flops 1088421888 | bytes 29361024 | tf_op jit(solution)/shard_map/while/body/eval_jaxpr/nab,ncb->nac/dot_general | solution.py:40
  222.9 92.2 %reduce-scatter.6.cloned.1.call-done = f32[16,128,128]{2,1,0:T(8,128)} async-done(((f32[128,128,128]{2,1,0:T(8,128)}), f32[16,128,128]{2,1,0:T(8,128)}) %reduce-scatter.6.cloned.1.call-update) | async-done | bytes 1048592 | tf_op jit(solution)/shard_map/reduce_scatter | solution.py:115
  317.2 14.3 %all-reduce.2 = (f32[]{:T(128)}, f32[]{:T(128)}, f32[]{:T(128)}) all-reduce(f32[]{:T(128)} %get-tuple-element.347, f32[]{:T(128)} %get-tuple-element.348, f32[]{:T(128)} %get-tuple-element.346), channel_id=1, replica_groups=mesh['seg'=4,'blk'=8] {'blk'}, use_global_device_ids=true, to_apply=%region_6.13 | all-reduce | flops 3 | bytes 24 | tf_op jit(solution)/shard_map/psum | solution.py:123
  342.8 10.3 collective-permute-done.7
  389.8 156.2 %while.37 = (s32[]{:T(128)}, f32[128,128,128]{2,1,0:T(8,128)}, f32[6,128]{1,0:T(8,128)S(1)}, bf16[6,8,128,128]{3,2,1,0:T(8,128)(2,1)S(1)}, s32[6,128]{1,0:T(8,12...) while((s32[]{:T(128)}, f32[128,128,128]{2,1,0:T(8,128)}, ...), condition=%wide.region_10.17_spmd.clone.clone, body=%wide.region_9.16_spmd.clone.clone.sunk | while | flops 1088431104 | bytes 55605624 | solution.py:45
  404.7 9.6 select_add_fusion.7
  429.2 11.4 %select_add_fusion.7 = f32[128,128,128]{2,1,0:T(8,128)} fusion(f32[128,128,128]{2,1,0:T(8,128)} %get-tuple-element.672, f32[128]{0:T(128)S(1)} %compare_select_fusion.32, pred[]{:T(512)S(6)} %compare.23, bf16[128,128,128]{2,1,0:T(8,128)(2,1)} %gather_fusion.6, pred[128]{0:T(512)(128)(4,1)S(1)} %get-tuple-element.611, ...), kind=kOutput, calls=%fused_computation.56.clone.1 | convolution fusion | flops 1088421888 | bytes 29361024 | tf_op jit(solution)/shard_map/while/body/eval_jaxpr/nab,ncb->nac/dot_general | solution.py:40
  455.5 11.4 %select_add_fusion.7 = f32[128,128,128]{2,1,0:T(8,128)} fusion(f32[128,128,128]{2,1,0:T(8,128)} %get-tuple-element.672, f32[128]{0:T(128)S(1)} %compare_select_fusion.32, pred[]{:T(512)S(6)} %compare.23, bf16[128,128,128]{2,1,0:T(8,128)(2,1)} %gather_fusion.6, pred[128]{0:T(512)(128)(4,1)S(1)} %get-tuple-element.611, ...), kind=kOutput, calls=%fused_computation.56.clone.1 | convolution fusion | flops 1088421888 | bytes 29361024 | tf_op jit(solution)/shard_map/while/body/eval_jaxpr/nab,ncb->nac/dot_general | solution.py:40
  481.8 11.4 %select_add_fusion.7 = f32[128,128,128]{2,1,0:T(8,128)} fusion(f32[128,128,128]{2,1,0:T(8,128)} %get-tuple-element.672, f32[128]{0:T(128)S(1)} %compare_select_fusion.32, pred[]{:T(512)S(6)} %compare.23, bf16[128,128,128]{2,1,0:T(8,128)(2,1)} %gather_fusion.6, pred[128]{0:T(512)(128)(4,1)S(1)} %get-tuple-element.611, ...), kind=kOutput, calls=%fused_computation.56.clone.1 | convolution fusion | flops 1088421888 | bytes 29361024 | tf_op jit(solution)/shard_map/while/body/eval_jaxpr/nab,ncb->nac/dot_general | solution.py:40
  508.2 11.4 %select_add_fusion.7 = f32[128,128,128]{2,1,0:T(8,128)} fusion(f32[128,128,128]{2,1,0:T(8,128)} %get-tuple-element.672, f32[128]{0:T(128)S(1)} %compare_select_fusion.32, pred[]{:T(512)S(6)} %compare.23, bf16[128,128,128]{2,1,0:T(8,128)(2,1)} %gather_fusion.6, pred[128]{0:T(512)(128)(4,1)S(1)} %get-tuple-element.611, ...), kind=kOutput, calls=%fused_computation.56.clone.1 | convolution fusion | flops 1088421888 | bytes 29361024 | tf_op jit(solution)/shard_map/while/body/eval_jaxpr/nab,ncb->nac/dot_general | solution.py:40
  534.5 11.4 %select_add_fusion.7 = f32[128,128,128]{2,1,0:T(8,128)} fusion(f32[128,128,128]{2,1,0:T(8,128)} %get-tuple-element.672, f32[128]{0:T(128)S(1)} %compare_select_fusion.32, pred[]{:T(512)S(6)} %compare.23, bf16[128,128,128]{2,1,0:T(8,128)(2,1)} %gather_fusion.6, pred[128]{0:T(512)(128)(4,1)S(1)} %get-tuple-element.611, ...), kind=kOutput, calls=%fused_computation.56.clone.1 | convolution fusion | flops 1088421888 | bytes 29361024 | tf_op jit(solution)/shard_map/while/body/eval_jaxpr/nab,ncb->nac/dot_general | solution.py:40
  546.0 87.8 %reduce-scatter.8.cloned.1.call-done = f32[16,128,128]{2,1,0:T(8,128)} async-done(((f32[128,128,128]{2,1,0:T(8,128)}), f32[16,128,128]{2,1,0:T(8,128)}) %reduce-scatter.8.cloned.1.call-update) | async-done | bytes 1048592 | tf_op jit(solution)/shard_map/reduce_scatter | solution.py:115
  635.9 14.4 %all-reduce.1 = (f32[]{:T(128)}, f32[]{:T(128)}, f32[]{:T(128)}) all-reduce(f32[]{:T(128)} %get-tuple-element.350, f32[]{:T(128)} %get-tuple-element.345, f32[]{:T(128)} %get-tuple-element.344), channel_id=1, replica_groups=mesh['seg'=4,'blk'=8] {'blk'}, use_global_device_ids=true, to_apply=%region_15.22 | all-reduce | flops 3 | bytes 24 | tf_op jit(solution)/shard_map/psum | solution.py:123
  661.6 10.3 collective-permute-done.14
  708.6 156.2 %while.38 = (s32[]{:T(128)}, f32[128,128,128]{2,1,0:T(8,128)}, f32[6,128]{1,0:T(8,128)S(1)}, bf16[6,8,128,128]{3,2,1,0:T(8,128)(2,1)S(1)}, s32[6,128]{1,0:T(8,12...) while((s32[]{:T(128)}, f32[128,128,128]{2,1,0:T(8,128)}, ...), condition=%wide.region_19.26_spmd.clone.clone, body=%wide.region_18.25_spmd.clone.clone.sunk | while | flops 1088431104 | bytes 55605624 | solution.py:45
  723.5 9.6 select_add_fusion.8
  748.0 11.4 %select_add_fusion.8 = f32[128,128,128]{2,1,0:T(8,128)} fusion(f32[128,128,128]{2,1,0:T(8,128)} %get-tuple-element.702, f32[128]{0:T(128)S(1)} %compare_select_fusion.34, pred[]{:T(512)S(6)} %compare.24, bf16[128,128,128]{2,1,0:T(8,128)(2,1)} %gather_fusion.11, pred[128]{0:T(512)(128)(4,1)S(1)} %get-tuple-element.626, ...), kind=kOutput, calls=%fused_computation.87.clone.1 | convolution fusion | flops 1088421888 | bytes 29361024 | tf_op jit(solution)/shard_map/while/body/eval_jaxpr/nab,ncb->nac/dot_general | solution.py:40
  774.3 11.4 %select_add_fusion.8 = f32[128,128,128]{2,1,0:T(8,128)} fusion(f32[128,128,128]{2,1,0:T(8,128)} %get-tuple-element.702, f32[128]{0:T(128)S(1)} %compare_select_fusion.34, pred[]{:T(512)S(6)} %compare.24, bf16[128,128,128]{2,1,0:T(8,128)(2,1)} %gather_fusion.11, pred[128]{0:T(512)(128)(4,1)S(1)} %get-tuple-element.626, ...), kind=kOutput, calls=%fused_computation.87.clone.1 | convolution fusion | flops 1088421888 | bytes 29361024 | tf_op jit(solution)/shard_map/while/body/eval_jaxpr/nab,ncb->nac/dot_general | solution.py:40
  800.7 11.4 %select_add_fusion.8 = f32[128,128,128]{2,1,0:T(8,128)} fusion(f32[128,128,128]{2,1,0:T(8,128)} %get-tuple-element.702, f32[128]{0:T(128)S(1)} %compare_select_fusion.34, pred[]{:T(512)S(6)} %compare.24, bf16[128,128,128]{2,1,0:T(8,128)(2,1)} %gather_fusion.11, pred[128]{0:T(512)(128)(4,1)S(1)} %get-tuple-element.626, ...), kind=kOutput, calls=%fused_computation.87.clone.1 | convolution fusion | flops 1088421888 | bytes 29361024 | tf_op jit(solution)/shard_map/while/body/eval_jaxpr/nab,ncb->nac/dot_general | solution.py:40
  827.0 11.4 %select_add_fusion.8 = f32[128,128,128]{2,1,0:T(8,128)} fusion(f32[128,128,128]{2,1,0:T(8,128)} %get-tuple-element.702, f32[128]{0:T(128)S(1)} %compare_select_fusion.34, pred[]{:T(512)S(6)} %compare.24, bf16[128,128,128]{2,1,0:T(8,128)(2,1)} %gather_fusion.11, pred[128]{0:T(512)(128)(4,1)S(1)} %get-tuple-element.626, ...), kind=kOutput, calls=%fused_computation.87.clone.1 | convolution fusion | flops 1088421888 | bytes 29361024 | tf_op jit(solution)/shard_map/while/body/eval_jaxpr/nab,ncb->nac/dot_general | solution.py:40
  853.3 11.4 %select_add_fusion.8 = f32[128,128,128]{2,1,0:T(8,128)} fusion(f32[128,128,128]{2,1,0:T(8,128)} %get-tuple-element.702, f32[128]{0:T(128)S(1)} %compare_select_fusion.34, pred[]{:T(512)S(6)} %compare.24, bf16[128,128,128]{2,1,0:T(8,128)(2,1)} %gather_fusion.11, pred[128]{0:T(512)(128)(4,1)S(1)} %get-tuple-element.626, ...), kind=kOutput, calls=%fused_computation.87.clone.1 | convolution fusion | flops 1088421888 | bytes 29361024 | tf_op jit(solution)/shard_map/while/body/eval_jaxpr/nab,ncb->nac/dot_general | solution.py:40
  864.8 87.8 %reduce-scatter.10.cloned.1.call-done = f32[16,128,128]{2,1,0:T(8,128)} async-done(((f32[128,128,128]{2,1,0:T(8,128)}), f32[16,128,128]{2,1,0:T(8,128)}) %reduce-scatter.10.cloned.1.call-update) | async-done | bytes 1048592 | tf_op jit(solution)/shard_map/reduce_scatter | solution.py:115
  954.7 14.5 %all-reduce = (f32[]{:T(128)}, f32[]{:T(128)}, f32[]{:T(128)}) all-reduce(f32[]{:T(128)} %get-tuple-element.349, f32[]{:T(128)} %get-tuple-element.343, f32[]{:T(128)} %get-tuple-element.342), channel_id=1, replica_groups=mesh['seg'=4,'blk'=8] {'blk'}, use_global_device_ids=true, to_apply=%region_24.31 | all-reduce | flops 3 | bytes 24 | tf_op jit(solution)/shard_map/psum | solution.py:123
  982.3 25.2 %reduce-scatter.14.cloned.1.call-done = f32[128,128]{1,0:T(8,128)} async-done(((f32[1024,128]{1,0:T(8,128)}), f32[128,128]{1,0:T(8,128)}) %reduce-scatter.14.cloned.1.call-update) | async-done | bytes 65552 | tf_op jit(solution)/shard_map/reduce_scatter | solution.py:133
  1010.9 28.1 %reduce-scatter.12.cloned.1.call-done = f32[128,128]{1,0:T(8,128)} async-done(((f32[1024,128]{1,0:T(8,128)}), f32[128,128]{1,0:T(8,128)}) %reduce-scatter.12.cloned.1.call-update) | async-done | bytes 65552 | tf_op jit(solution)/shard_map/reduce_scatter | solution.py:132
  (450 shorter events, 425.5 us)
Async XLA Ops:
  7.2 307.9 %reduce-scatter.6.cloned.1.call-start = ((), (), s32[]{:S(2)}) async-start(), calls=%async_computation.5 | async-start | bytes 9437184 | tf_op jit(solution)/shard_map/reduce_scatter | solution.py:115
  8.8 34.9 %copy-start.11 = (s32[1,6,128]{2,0,1:T(1,128)S(1)}, s32[1,6,128]{2,0,1:T(1,128)}, u32[]{:S(2)}) copy-start(s32[1,6,128]{2,0,1:T(1,128)} %param.30) | copy-start | bytes 9220
  8.8 34.9 %copy-start.12 = (f32[1,6,128]{2,0,1:T(1,128)S(1)}, f32[1,6,128]{2,0,1:T(1,128)}, u32[]{:S(2)}) copy-start(f32[1,6,128]{2,0,1:T(1,128)} %param.29) | copy-start | bytes 9220
  15.4 50.6 %copy-start.1 = (bf16[1,6,8,128,128]{4,3,2,1,0:T(8,128)(2,1)S(1)}, bf16[1,6,8,128,128]{4,3,2,1,0:T(8,128)(2,1)}, u32[]{:S(2)}) copy-start(bf16[1,6,8,128,128]{4,3,2,1,0:T(8,128)(2,1)} %param.27) | copy-start | bytes 4718596
  15.4 14.5 %collective-permute-start = (bf16[16,128,128]{2,1,0:T(8,128)(2,1)S(1)}, bf16[16,128,128]{2,1,0:T(8,128)(2,1)S(1)}, u32[]{:S(2)}, u32[]{:S(2)}) collective-permute-start(bf16[16,128,128]{2,1,0:T(8,128)(2,1)S(1)} %get-tuple-element.421), channel_id=1, source_target_pairs={{0,1},{1,2},{2,3},{3,4},{4,5},{5,6},{6,7},{7,0},{8,9},{9,10},{10,1... | collective-permute-start | bytes 1572872 | tf_op jit(solution)/shard_map/ppermute | solution.py:98
  15.9 14.3 %collective-permute-start.1 = (bf16[16,128,128]{2,1,0:T(8,128)(2,1)S(1)}, bf16[16,128,128]{2,1,0:T(8,128)(2,1)}, u32[]{:S(2)}, u32[]{:S(2)}) collective-permute-start(bf16[16,128,128]{2,1,0:T(8,128)(2,1)S(1)} %get-tuple-element.421), channel_id=1, source_target_pairs={{0,7},{1,0},{2,1},{3,2},{4,3},{5,4},{6,5},{7,6},{8,15},{9,8},{10,9... | collective-permute-start | bytes 1572872 | tf_op jit(solution)/shard_map/ppermute | solution.py:103
  29.9 12.6 %collective-permute-start.2 = (bf16[16,128,128]{2,1,0:T(8,128)(2,1)S(1)}, bf16[16,128,128]{2,1,0:T(8,128)(2,1)}, u32[]{:S(2)}, u32[]{:S(2)}) collective-permute-start(bf16[16,128,128]{2,1,0:T(8,128)(2,1)S(1)} %collective-permute-done), channel_id=1, source_target_pairs={{0,1},{1,2},{2,3},{3,4},{4,5},{5,6},{6,7},{7,0},{8,9},{9,10},{10,1... | collective-permute-start | bytes 1572872 | tf_op jit(solution)/shard_map/ppermute | solution.py:98
  30.6 13.1 %collective-permute-start.3 = (bf16[16,128,128]{2,1,0:T(8,128)(2,1)}, bf16[16,128,128]{2,1,0:T(8,128)(2,1)}, u32[]{:S(2)}, u32[]{:S(2)}) collective-permute-start(bf16[16,128,128]{2,1,0:T(8,128)(2,1)} %collective-permute-done.1), channel_id=1, source_target_pairs={{0,7},{1,0},{2,1},{3,2},{4,3},{5,4},{6,5},{7,6},{8,15},{9,8},{10,9... | collective-permute-start | bytes 1572872 | tf_op jit(solution)/shard_map/ppermute | solution.py:103
  42.5 10.8 %collective-permute-start.4 = (bf16[16,128,128]{2,1,0:T(8,128)(2,1)}, bf16[16,128,128]{2,1,0:T(8,128)(2,1)}, u32[]{:S(2)}, u32[]{:S(2)}) collective-permute-start(bf16[16,128,128]{2,1,0:T(8,128)(2,1)} %collective-permute-done.2), channel_id=1, source_target_pairs={{0,1},{1,2},{2,3},{3,4},{4,5},{5,6},{6,7},{7,0},{8,9},{9,10},{10,1... | collective-permute-start | bytes 1572872 | tf_op jit(solution)/shard_map/ppermute | solution.py:98
  43.8 17.0 %collective-permute-start.5 = (bf16[16,128,128]{2,1,0:T(8,128)(2,1)}, bf16[16,128,128]{2,1,0:T(8,128)(2,1)S(1)}, u32[]{:S(2)}, u32[]{:S(2)}) collective-permute-start(bf16[16,128,128]{2,1,0:T(8,128)(2,1)} %collective-permute-done.3), channel_id=1, source_target_pairs={{0,7},{1,0},{2,1},{3,2},{4,3},{5,4},{6,5},{7,6},{8,15},{9,8},{10,9... | collective-permute-start | bytes 1572872 | tf_op jit(solution)/shard_map/ppermute | solution.py:103
  53.3 11.9 %collective-permute-start.6 = (bf16[16,128,128]{2,1,0:T(8,128)(2,1)}, bf16[16,128,128]{2,1,0:T(8,128)(2,1)S(1)}, u32[]{:S(2)}, u32[]{:S(2)}) collective-permute-start(bf16[16,128,128]{2,1,0:T(8,128)(2,1)} %collective-permute-done.4), channel_id=1, source_target_pairs={{0,1},{1,2},{2,3},{3,4},{4,5},{5,6},{6,7},{7,0},{8,9},{9,10},{10,1... | collective-permute-start | bytes 1572872 | tf_op jit(solution)/shard_map/ppermute | solution.py:98
  222.2 411.6 %reduce-scatter.8.cloned.1.call-start = ((), (), s32[]{:S(2)}) async-start(), calls=%async_computation.6 | async-start | bytes 9437184 | tf_op jit(solution)/shard_map/reduce_scatter | solution.py:115
  339.2 294.5 %copy-start.2 = (f32[16,128,128]{2,1,0:T(8,128)}, f32[16,128,128]{2,1,0:T(8,128)S(1)}, u32[]{:S(2)}) copy-start(f32[16,128,128]{2,1,0:T(8,128)S(1)} %get-tuple-element.419) | copy-start | bytes 3145732
  339.2 13.8 %collective-permute-start.7 = (bf16[16,128,128]{2,1,0:T(8,128)(2,1)S(1)}, bf16[16,128,128]{2,1,0:T(8,128)(2,1)S(1)}, u32[]{:S(2)}, u32[]{:S(2)}) collective-permute-start(bf16[16,128,128]{2,1,0:T(8,128)(2,1)S(1)} %get-tuple-element.418), channel_id=1, source_target_pairs={{0,1},{1,2},{2,3},{3,4},{4,5},{5,6},{6,7},{7,0},{8,9},{9,10},{10,1... | collective-permute-start | bytes 1572872 | tf_op jit(solution)/shard_map/ppermute | solution.py:98
  339.2 13.8 %collective-permute-start.8 = (bf16[16,128,128]{2,1,0:T(8,128)(2,1)S(1)}, bf16[16,128,128]{2,1,0:T(8,128)(2,1)S(1)}, u32[]{:S(2)}, u32[]{:S(2)}) collective-permute-start(bf16[16,128,128]{2,1,0:T(8,128)(2,1)S(1)} %get-tuple-element.418), channel_id=1, source_target_pairs={{0,7},{1,0},{2,1},{3,2},{4,3},{5,4},{6,5},{7,6},{8,15},{9,8},{10,9... | collective-permute-start | bytes 1572872 | tf_op jit(solution)/shard_map/ppermute | solution.py:103
  353.0 12.6 %collective-permute-start.9 = (bf16[16,128,128]{2,1,0:T(8,128)(2,1)S(1)}, bf16[16,128,128]{2,1,0:T(8,128)(2,1)}, u32[]{:S(2)}, u32[]{:S(2)}) collective-permute-start(bf16[16,128,128]{2,1,0:T(8,128)(2,1)S(1)} %collective-permute-done.7), channel_id=1, source_target_pairs={{0,1},{1,2},{2,3},{3,4},{4,5},{5,6},{6,7},{7,0},{8,9},{9,10},{10,1... | collective-permute-start | bytes 1572872 | tf_op jit(solution)/shard_map/ppermute | solution.py:98
  353.8 13.1 %collective-permute-start.10 = (bf16[16,128,128]{2,1,0:T(8,128)(2,1)S(1)}, bf16[16,128,128]{2,1,0:T(8,128)(2,1)}, u32[]{:S(2)}, u32[]{:S(2)}) collective-permute-start(bf16[16,128,128]{2,1,0:T(8,128)(2,1)S(1)} %collective-permute-done.8), channel_id=1, source_target_pairs={{0,7},{1,0},{2,1},{3,2},{4,3},{5,4},{6,5},{7,6},{8,15},{9,8},{10,9... | collective-permute-start | bytes 1572872 | tf_op jit(solution)/shard_map/ppermute | solution.py:103
  365.6 12.7 %collective-permute-start.11 = (bf16[16,128,128]{2,1,0:T(8,128)(2,1)}, bf16[16,128,128]{2,1,0:T(8,128)(2,1)}, u32[]{:S(2)}, u32[]{:S(2)}) collective-permute-start(bf16[16,128,128]{2,1,0:T(8,128)(2,1)} %collective-permute-done.9), channel_id=1, source_target_pairs={{0,1},{1,2},{2,3},{3,4},{4,5},{5,6},{6,7},{7,0},{8,9},{9,10},{10,1... | collective-permute-start | bytes 1572872 | tf_op jit(solution)/shard_map/ppermute | solution.py:98
  367.0 17.9 %collective-permute-start.12 = (bf16[16,128,128]{2,1,0:T(8,128)(2,1)}, bf16[16,128,128]{2,1,0:T(8,128)(2,1)S(1)}, u32[]{:S(2)}, u32[]{:S(2)}) collective-permute-start(bf16[16,128,128]{2,1,0:T(8,128)(2,1)} %collective-permute-done.10), channel_id=1, source_target_pairs={{0,7},{1,0},{2,1},{3,2},{4,3},{5,4},{6,5},{7,6},{8,15},{9,8},{10,9... | collective-permute-start | bytes 1572872 | tf_op jit(solution)/shard_map/ppermute | solution.py:103
  378.3 10.6 %collective-permute-start.13 = (bf16[16,128,128]{2,1,0:T(8,128)(2,1)}, bf16[16,128,128]{2,1,0:T(8,128)(2,1)S(1)}, u32[]{:S(2)}, u32[]{:S(2)}) collective-permute-start(bf16[16,128,128]{2,1,0:T(8,128)(2,1)} %collective-permute-done.11), channel_id=1, source_target_pairs={{0,1},{1,2},{2,3},{3,4},{4,5},{5,6},{6,7},{7,0},{8,9},{9,10},{10,1... | collective-permute-start | bytes 1572872 | tf_op jit(solution)/shard_map/ppermute | solution.py:98
  546.0 406.7 %reduce-scatter.10.cloned.1.call-start = ((), (), s32[]{:S(2)}) async-start(), calls=%async_computation.7 | async-start | bytes 9437184 | tf_op jit(solution)/shard_map/reduce_scatter | solution.py:115
  658.1 13.8 %collective-permute-start.14 = (bf16[16,128,128]{2,1,0:T(8,128)(2,1)S(1)}, bf16[16,128,128]{2,1,0:T(8,128)(2,1)S(1)}, u32[]{:S(2)}, u32[]{:S(2)}) collective-permute-start(bf16[16,128,128]{2,1,0:T(8,128)(2,1)S(1)} %get-tuple-element.415), channel_id=1, source_target_pairs={{0,1},{1,2},{2,3},{3,4},{4,5},{5,6},{6,7},{7,0},{8,9},{9,10},{10,1... | collective-permute-start | bytes 1572872 | tf_op jit(solution)/shard_map/ppermute | solution.py:98
  658.1 13.8 %collective-permute-start.15 = (bf16[16,128,128]{2,1,0:T(8,128)(2,1)S(1)}, bf16[16,128,128]{2,1,0:T(8,128)(2,1)S(1)}, u32[]{:S(2)}, u32[]{:S(2)}) collective-permute-start(bf16[16,128,128]{2,1,0:T(8,128)(2,1)S(1)} %get-tuple-element.415), channel_id=1, source_target_pairs={{0,7},{1,0},{2,1},{3,2},{4,3},{5,4},{6,5},{7,6},{8,15},{9,8},{10,9... | collective-permute-start | bytes 1572872 | tf_op jit(solution)/shard_map/ppermute | solution.py:103
  671.9 12.6 %collective-permute-start.16 = (bf16[16,128,128]{2,1,0:T(8,128)(2,1)S(1)}, bf16[16,128,128]{2,1,0:T(8,128)(2,1)}, u32[]{:S(2)}, u32[]{:S(2)}) collective-permute-start(bf16[16,128,128]{2,1,0:T(8,128)(2,1)S(1)} %collective-permute-done.14), channel_id=1, source_target_pairs={{0,1},{1,2},{2,3},{3,4},{4,5},{5,6},{6,7},{7,0},{8,9},{9,10},{10,1... | collective-permute-start | bytes 1572872 | tf_op jit(solution)/shard_map/ppermute | solution.py:98
  672.6 13.1 %collective-permute-start.17 = (bf16[16,128,128]{2,1,0:T(8,128)(2,1)S(1)}, bf16[16,128,128]{2,1,0:T(8,128)(2,1)}, u32[]{:S(2)}, u32[]{:S(2)}) collective-permute-start(bf16[16,128,128]{2,1,0:T(8,128)(2,1)S(1)} %collective-permute-done.15), channel_id=1, source_target_pairs={{0,7},{1,0},{2,1},{3,2},{4,3},{5,4},{6,5},{7,6},{8,15},{9,8},{10,9... | collective-permute-start | bytes 1572872 | tf_op jit(solution)/shard_map/ppermute | solution.py:103
  684.4 12.7 %collective-permute-start.18 = (bf16[16,128,128]{2,1,0:T(8,128)(2,1)}, bf16[16,128,128]{2,1,0:T(8,128)(2,1)}, u32[]{:S(2)}, u32[]{:S(2)}) collective-permute-start(bf16[16,128,128]{2,1,0:T(8,128)(2,1)} %collective-permute-done.16), channel_id=1, source_target_pairs={{0,1},{1,2},{2,3},{3,4},{4,5},{5,6},{6,7},{7,0},{8,9},{9,10},{10,1... | collective-permute-start | bytes 1572872 | tf_op jit(solution)/shard_map/ppermute | solution.py:98
  685.8 17.9 %collective-permute-start.19 = (bf16[16,128,128]{2,1,0:T(8,128)(2,1)}, bf16[16,128,128]{2,1,0:T(8,128)(2,1)S(1)}, u32[]{:S(2)}, u32[]{:S(2)}) collective-permute-start(bf16[16,128,128]{2,1,0:T(8,128)(2,1)} %collective-permute-done.17), channel_id=1, source_target_pairs={{0,7},{1,0},{2,1},{3,2},{4,3},{5,4},{6,5},{7,6},{8,15},{9,8},{10,9... | collective-permute-start | bytes 1572872 | tf_op jit(solution)/shard_map/ppermute | solution.py:103
  697.1 10.6 %collective-permute-start.20 = (bf16[16,128,128]{2,1,0:T(8,128)(2,1)}, bf16[16,128,128]{2,1,0:T(8,128)(2,1)S(1)}, u32[]{:S(2)}, u32[]{:S(2)}) collective-permute-start(bf16[16,128,128]{2,1,0:T(8,128)(2,1)} %collective-permute-done.18), channel_id=1, source_target_pairs={{0,1},{1,2},{2,3},{3,4},{4,5},{5,6},{6,7},{7,0},{8,9},{9,10},{10,1... | collective-permute-start | bytes 1572872 | tf_op jit(solution)/shard_map/ppermute | solution.py:98
  864.8 142.8 %reduce-scatter.14.cloned.1.call-start = ((), (), s32[]{:S(2)}) async-start(), calls=%async_computation.9 | async-start | bytes 589824 | tf_op jit(solution)/shard_map/reduce_scatter | solution.py:133
  952.6 23.3 %copy-start.14 = (s32[16]{0:T(128)S(1)}, s32[16]{0:T(128)}, u32[]{:S(2)}) copy-start(s32[16]{0:T(128)} %copy-done.13) | copy-start | bytes 196
  978.0 61.1 %reduce-scatter.12.cloned.1.call-start = ((), (), s32[]{:S(2)}) async-start(), calls=%async_computation.8 | async-start | bytes 589824 | tf_op jit(solution)/shard_map/reduce_scatter | solution.py:132
  1007.6 31.5 %collective-permute-start.21 = (f32[128,128]{1,0:T(8,128)}, f32[128,128]{1,0:T(8,128)S(1)}, u32[]{:S(2)}, u32[]{:S(2)}) collective-permute-start(f32[128,128]{1,0:T(8,128)} %reduce-scatter.14.cloned.1.call-done), channel_id=1, source_target_pairs={{0,8},{8,16},{16,24},{1,9},{9,17},{17,25},{2,10},{10,18},{18,26},{... | collective-permute-start | bytes 196616 | tf_op jit(solution)/shard_map/ppermute | solution.py:16
  (10 other events, 29.5 us)
Sparse Core Ops, SparseCore 0:
  222.3 92.7 reduce-scatter.5
  546.1 87.6 reduce-scatter.7
  864.9 87.6 reduce-scatter.9
  978.1 29.4 reduce-scatter.13
  1009.7 29.3 reduce-scatter.11
